TPU v7x, 32 devices: a whole 2x2x4 slice. The times are simulated.
32 devices in a mesh: gx: 4 (over z), gy: 8 (over y, x, core).
Axes of the slice: x: 2, y: 2, z: 4, core: 2. Of those that a mesh axis runs over, the one named last changes fastest.
Arguments:
- velocity: float32 [3, 32, 64, 1024], P(None, None, 'gx', 'gy'), may hold values from -6 to 6
- old_tendency: float32 [3, 32, 64, 1024], P(None, None, 'gx', 'gy'), may hold values from -6 to 6
- obstacle: int32 [32, 64, 1024], P(None, 'gx', 'gy'), may hold values 0 or 1
Outputs:
- corrected: float32 [3, 32, 64, 1024], P(None, None, 'gx', 'gy')
- pressure: float32 [32, 64, 1024], P(None, 'gx', 'gy')
Inputs may be any that keep to these rules, and one draw needn't show every extreme that they name: `obstacle`: 1 marks a building cell, 0 a fluid cell.
All inputs are finite; a program needn't handle non-finite values. No bound on the sum of `obstacle` on one device may be relied on, other than what follows from the above.
Results may differ from a plain program's by a relative error of at most 0.00002.
Values sent between devices are 32-bit elements; how exact they have to be, the bound alone decides.
A program may use at most 128 MiB of HBM per device.

v0:
```python
import jax
import jax.numpy as jnp
from jax import lax
from jax.sharding import PartitionSpec as P

LEVELS = 3
SWEEPS = 2
COARSE_SWEEPS = 8


VISCOSITY = 0.1
TIME_STEP = 0.25
WEIGHT_NEW = 15.0 / 16.0
WEIGHT_OLD = -25.0 / 48.0
HELMHOLTZ = 0.0001


def extended_2(block, sides, width):
    for axis, dim in sides:
        count = lax.axis_size(axis)
        forward = [(i, i + 1) for i in range(count - 1)]
        forward.append((count - 1, 0))
        backward = [(target, source) for source, target in forward]
        low = lax.ppermute(
            lax.slice_in_dim(block, block.shape[dim] - width, None, axis=dim), axis, forward
        )
        high = lax.ppermute(lax.slice_in_dim(block, 0, width, axis=dim), axis, backward)
        block = jnp.concatenate([low, block, high], axis=dim)
    return block


def vertical_pair(field):
    zeros_layer = jnp.zeros_like(field[..., :1, :, :])
    upper_cell = jnp.concatenate([field[..., 1:, :, :], zeros_layer], axis=-3)
    lower_cell = jnp.concatenate([zeros_layer, field[..., :-1, :, :]], axis=-3)
    return (upper_cell, lower_cell)


def vertical_count(size_z):
    layers = jnp.arange(size_z)
    above_ok = (layers < size_z - 1).astype(jnp.float32)
    below_ok = (layers > 0).astype(jnp.float32)
    return (above_ok + below_ok)[:, None, None]


def parity(size_z, size_x, size_y, start_x, start_y):
    layer_z = jnp.arange(size_z, dtype=jnp.int32)[:, None, None]
    row_x = (jnp.arange(size_x, dtype=jnp.int32) + start_x)[None, :, None]
    col_y = (jnp.arange(size_y, dtype=jnp.int32) + start_y)[None, None, :]
    return (layer_z + row_x + col_y) % 2


def gather_neighbours(extended):
    center = extended[:, 1:-1, 1:-1]
    upper_cell, lower_cell = vertical_pair(center)
    neighbours = (
        extended[:, 2:, 1:-1]
        + extended[:, :-2, 1:-1]
        + extended[:, 1:-1, 2:]
        + extended[:, 1:-1, :-2]
        + upper_cell
        + lower_cell
    )
    return (center, neighbours)


def relax_update(extended, source, spacing):
    center, neighbours = gather_neighbours(extended)
    diagonal = HELMHOLTZ + (4.0 + vertical_count(center.shape[0])) / spacing
    return (source + neighbours / spacing) / diagonal


def apply_operator(extended, spacing):
    center, neighbours = gather_neighbours(extended)
    diagonal = HELMHOLTZ + (4.0 + vertical_count(center.shape[0])) / spacing
    return diagonal * center - neighbours / spacing


def wrapped(field):
    return jnp.pad(field, ((0, 0), (1, 1), (1, 1)), mode="wrap")


def restrict(field):
    size_z, size_x, size_y = field.shape
    return field.reshape(size_z // 2, 2, size_x // 2, 2, size_y // 2, 2).mean(axis=(1, 3, 5))


def prolong(field):
    return jnp.repeat(jnp.repeat(jnp.repeat(field, 2, axis=0), 2, axis=1), 2, axis=2)


def global_sweep(field, source, spacing, colour):
    for shade in (0, 1):
        field = jnp.where(colour == shade, relax_update(wrapped(field), source, spacing), field)
    return field


def global_cycle(source, level):
    spacing = float(4**level)
    size_z, size_x, size_y = source.shape
    colour = parity(size_z, size_x, size_y, 0, 0)
    field = jnp.zeros_like(source)
    if level == LEVELS:
        for repeat_idx in range(COARSE_SWEEPS):
            field = global_sweep(field, source, spacing, colour)
        return field
    for repeat_idx in range(SWEEPS):
        field = global_sweep(field, source, spacing, colour)
    remain = source - apply_operator(wrapped(field), spacing)
    field = field + prolong(global_cycle(restrict(remain), level + 1))
    for repeat_idx in range(SWEEPS):
        field = global_sweep(field, source, spacing, colour)
    return field


def momentum(velocity, plus_x, minus_x, plus_y, minus_y, old_tendency, fluid):
    upper_cell, lower_cell = vertical_pair(velocity)
    advect = (
        velocity[0] * (plus_x - minus_x) * 0.5
        + velocity[1] * (plus_y - minus_y) * 0.5
        + velocity[2] * (upper_cell - lower_cell) * 0.5
    )
    diffuse = plus_x + minus_x + plus_y + minus_y + upper_cell + lower_cell - 6.0 * velocity
    tendency = VISCOSITY * diffuse - advect
    return fluid * (velocity + TIME_STEP * (WEIGHT_NEW * tendency + WEIGHT_OLD * old_tendency))


def divergence_of(east_u, west_u, north_v, south_v, predicted):
    upper_cell, lower_cell = vertical_pair(predicted[2])
    return 0.5 * (east_u - west_u + (north_v - south_v) + (upper_cell - lower_cell))


def correct(predicted, pressure_ext, pressure, fluid):
    upper_cell, lower_cell = vertical_pair(pressure)
    gradient = jnp.stack(
        [
            0.5 * (pressure_ext[:, 2:, 1:-1] - pressure_ext[:, :-2, 1:-1]),
            0.5 * (pressure_ext[:, 1:-1, 2:] - pressure_ext[:, 1:-1, :-2]),
            0.5 * (upper_cell - lower_cell),
        ]
    )
    return fluid * (predicted - TIME_STEP * gradient)


def face_halo(field):
    return extended_2(field, (("gx", 1), ("gy", 2)), 1)


def smooth(field, source, spacing, colour):
    for shade in (0, 1):
        field = jnp.where(colour == shade, relax_update(face_halo(field), source, spacing), field)
    return field


def agglomerated(source, level, index_x, index_y):
    size_z, size_x, size_y = source.shape
    stacked = lax.all_gather(source[None], ("gx", "gy"), axis=0, tiled=True)
    count_x = lax.axis_size("gx")
    count_y = lax.axis_size("gy")
    whole_grid = stacked.reshape(count_x, count_y, size_z, size_x, size_y).transpose(2, 0, 3, 1, 4)
    whole_grid = whole_grid.reshape(size_z, count_x * size_x, count_y * size_y)
    solved = global_cycle(whole_grid, level)
    anchor = (jnp.int32(0), index_x * size_x, index_y * size_y)
    return lax.dynamic_slice(solved, anchor, (size_z, size_x, size_y))


def local_cycle(source, level, index_x, index_y):
    stop_level = LEVELS - 1
    if level == stop_level:
        return agglomerated(source, level, index_x, index_y)
    size_z, size_x, size_y = source.shape
    spacing = float(4**level)
    start_x = index_x * size_x
    start_y = index_y * size_y
    colour = parity(size_z, size_x, size_y, start_x, start_y)
    field = jnp.zeros_like(source)
    for repeat_idx in range(SWEEPS):
        field = smooth(field, source, spacing, colour)
    remain = source - apply_operator(face_halo(field), spacing)
    field = field + prolong(local_cycle(restrict(remain), level + 1, index_x, index_y))
    for repeat_idx in range(SWEEPS):
        field = smooth(field, source, spacing, colour)
    return field


def body(velocity, old_tendency, obstacle):
    fluid = (1 - obstacle).astype(jnp.float32)
    components, size_z, size_x, size_y = velocity.shape
    extended = face_halo(velocity.reshape(components * size_z, size_x, size_y))
    extended = extended.reshape(components, size_z, size_x + 2, size_y + 2)
    predicted = momentum(
        velocity,
        extended[:, :, 2:, 1:-1],
        extended[:, :, :-2, 1:-1],
        extended[:, :, 1:-1, 2:],
        extended[:, :, 1:-1, :-2],
        old_tendency,
        fluid,
    )
    rims_east = extended_2(predicted[0], (("gx", 1),), 1)
    rims_north = extended_2(predicted[1], (("gy", 2),), 1)
    divergence = divergence_of(
        rims_east[:, 2:, :],
        rims_east[:, :-2, :],
        rims_north[:, :, 2:],
        rims_north[:, :, :-2],
        predicted,
    )
    source = -divergence / TIME_STEP
    index_x = lax.axis_index("gx")
    index_y = lax.axis_index("gy")
    pressure = local_cycle(source, 0, index_x, index_y)
    corrected = correct(predicted, face_halo(pressure), pressure, fluid)
    return (corrected, pressure)


def solution(mesh):
    placed = (P(None, None, "gx", "gy"), P(None, None, "gx", "gy"), P(None, "gx", "gy"))
    return jax.shard_map(
        body,
        mesh=mesh,
        in_specs=placed,
        out_specs=(P(None, None, "gx", "gy"), P(None, "gx", "gy")),
        check_vma=False,
    )
```

profile of v0, /device:TPU:0, one launch (start us, length us, event | category | flops | bytes accessed | tf_op | source)
XLA Modules:
  0.0 369.1 jit_solution(16207955259812831852)
XLA Ops:
  0.6 5.1 %collective-permute-start.8 = (f32[32,1,128]{2,0,1:T(8,128)S(1)}, f32[32,1,128]{2,0,1:T(8,128)S(1)}, u32[]{:S(2)}, u32[]{:S(2)}) collective-permute-start(f32[32,1,128]{2,0,1:T(8,128)S(1)} %broadcast.525), channel_id=1, source_target_pairs={{8,0},{16,8},{24,16},{0,24},{9,1},{17,9},{25,17},{1,25},{10,2},{18... | collective-permute-start | bytes 49160 | tf_op jit(solution)/shard_map/ppermute | solution.py:27
  7.3 3.9 %collective-permute-start.1 = (f32[96,1,128]{2,0,1:T(8,128)S(1)}, f32[96,1,128]{2,0,1:T(8,128)S(1)}, u32[]{:S(2)}, u32[]{:S(2)}) collective-permute-start(f32[96,1,128]{2,0,1:T(8,128)S(1)} %get-tuple-element.24), channel_id=1, source_target_pairs={{8,0},{16,8},{24,16},{0,24},{9,1},{17,9},{25,17},{1,25},{10,2},{18... | collective-permute-start | bytes 147464 | tf_op jit(solution)/shard_map/ppermute | solution.py:27
  21.4 2.7 collective-permute-start.3
  27.1 2.1 pad_maximum_fusion
  30.7 2.3 collective-permute-start.6
  35.1 3.8 %collective-permute-start.28 = (f32[16,1,64]{2,1,0:T(1,128)S(1)}, f32[16,1,64]{2,1,0:T(1,128)S(1)}, u32[]{:S(2)}, u32[]{:S(2)}) collective-permute-start(f32[16,1,64]{2,1,0:T(1,128)S(1)} %broadcast.529), channel_id=1, source_target_pairs={{8,0},{16,8},{24,16},{0,24},{9,1},{17,9},{25,17},{1,25},{10,2},{18... | collective-permute-start | bytes 12296 | tf_op jit(solution)/shard_map/ppermute | solution.py:27
  46.2 3.7 %collective-permute-done.13 = f32[32,1,128]{2,0,1:T(8,128)S(1)} collective-permute-done((f32[32,1,128]{2,0,1:T(8,128)S(1)}, f32[32,1,128]{2,0,1:T(8,128)S(1)}, u32[]{:S(2)}, u32[]{:S(2)}) %collective-permute-start.13) | collective-permute-done | bytes 16416 | tf_op jit(solution)/shard_map/ppermute | solution.py:24
  51.3 6.4 %collective-permute-done.14 = f32[32,18,1]{2,0,1:T(8,128)S(1)} collective-permute-done((f32[32,18,1]{2,0,1:T(8,128)S(1)}, f32[32,18,1]{2,0,1:T(8,128)S(1)}, u32[]{:S(2)}, u32[]{:S(2)}) %collective-permute-start.14) | collective-permute-done | bytes 2336 | tf_op jit(solution)/shard_map/ppermute | solution.py:27
  65.7 6.5 %collective-permute-done.18 = f32[32,18,1]{2,0,1:T(8,128)S(1)} collective-permute-done((f32[32,18,1]{2,0,1:T(8,128)S(1)}, f32[32,18,1]{2,0,1:T(8,128)S(1)}, u32[]{:S(2)}, u32[]{:S(2)}) %collective-permute-start.18) | collective-permute-done | bytes 2336 | tf_op jit(solution)/shard_map/ppermute | solution.py:27
  80.6 6.7 %collective-permute-done.22 = f32[32,18,1]{2,0,1:T(8,128)S(1)} collective-permute-done((f32[32,18,1]{2,0,1:T(8,128)S(1)}, f32[32,18,1]{2,0,1:T(8,128)S(1)}, u32[]{:S(2)}, u32[]{:S(2)}) %collective-permute-start.22) | collective-permute-done | bytes 2336 | tf_op jit(solution)/shard_map/ppermute | solution.py:27
  93.0 2.9 collective-permute-done.25
  96.7 6.7 %collective-permute-done.26 = f32[32,18,1]{2,0,1:T(8,128)S(1)} collective-permute-done((f32[32,18,1]{2,0,1:T(8,128)S(1)}, f32[32,18,1]{2,0,1:T(8,128)S(1)}, u32[]{:S(2)}, u32[]{:S(2)}) %collective-permute-start.26) | collective-permute-done | bytes 2336 | tf_op jit(solution)/shard_map/ppermute | solution.py:27
  104.5 18.1 %reshape.216 = f32[16,2,8,2,64,2]{5,4,3,2,1,0:T(8,128)} reshape(f32[32,16,128]{2,1,0:T(8,128)S(1)} %copy.318) | data formatting | bytes 524288 | tf_op jit(solution)/shard_map/reshape | solution.py:85
  122.6 7.0 %reduce_sum.27 = f32[16,8,64]{2,1,0:T(8,128)S(1)} reduce(f32[16,2,8,2,64,2]{5,4,3,2,1,0:T(8,128)} %reshape.216, f32[]{:T(128)} %constant.84.clone.1), dimensions={1,3,5}, to_apply=%region_0.1 | reduce | flops 57344 | bytes 294916 | tf_op jit(solution)/shard_map/reduce_sum | solution.py:85
  129.9 3.7 collective-permute-start.32
  136.4 2.7 collective-permute-done.34
  139.1 2.1 collective-permute-done.35
  141.5 3.8 %collective-permute-start.36 = (f32[16,1,64]{2,1,0:T(1,128)S(1)}, f32[16,1,64]{2,1,0:T(1,128)S(1)}, u32[]{:S(2)}, u32[]{:S(2)}) collective-permute-start(f32[16,1,64]{2,1,0:T(1,128)S(1)} %get-tuple-element.201), channel_id=1, source_target_pairs={{8,0},{16,8},{24,16},{0,24},{9,1},{17,9},{25,17},{1,25},{10,2},{18... | collective-permute-start | bytes 12296 | tf_op jit(solution)/shard_map/ppermute | solution.py:27
  147.6 2.3 collective-permute-done.38
  149.9 2.0 collective-permute-done.39
  153.1 3.0 collective-permute-start.40
  158.4 2.3 collective-permute-done.42
  164.2 2.8 collective-permute-start.44
  169.2 2.3 collective-permute-done.46
  171.5 2.1 collective-permute-done.47
  174.5 3.0 reshape.217
  177.8 42.0 %all-gather = f32[256,4,32]{2,1,0:T(4,128)S(1)} all-gather(f32[8,4,32]{2,1,0:T(4,128)S(1)} %broadcast_multiply_fusion.1), channel_id=2, replica_groups=mesh['gx'=4,'gy'=8] {'gx','gy'}, dimensions={0}, use_global_device_ids=true | all-gather | bytes 135168 | tf_op jit(solution)/shard_map/all_gather | solution.py:157
  222.0 9.7 %reshape.220 = f32[4,2,8,2,128,2]{5,4,3,2,1,0:T(8,128)} reshape(f32[8,16,256]{2,1,0:T(8,128)S(1)} %fusion.136) | data formatting | bytes 262144 | tf_op jit(solution)/shard_map/reshape | solution.py:85
  231.7 4.0 %reduce_sum.29 = f32[4,8,128]{2,1,0:T(8,128)S(1)} reduce(f32[4,2,8,2,128,2]{5,4,3,2,1,0:T(8,128)} %reshape.220, f32[]{:T(128)} %constant.84.clone.1), dimensions={1,3,5}, to_apply=%region_2.3 | reduce | flops 28672 | bytes 147460 | tf_op jit(solution)/shard_map/reduce_sum | solution.py:85
  243.1 3.8 %collective-permute-start.48 = (f32[16,1,64]{2,1,0:T(1,128)S(1)}, f32[16,1,64]{2,1,0:T(1,128)S(1)}, u32[]{:S(2)}, u32[]{:S(2)}) collective-permute-start(f32[16,1,64]{2,1,0:T(1,128)S(1)} %get-tuple-element.189), channel_id=1, source_target_pairs={{8,0},{16,8},{24,16},{0,24},{9,1},{17,9},{25,17},{1,25},{10,2},{18... | collective-permute-start | bytes 12296 | tf_op jit(solution)/shard_map/ppermute | solution.py:27
  249.2 2.1 collective-permute-done.50
  251.3 2.2 collective-permute-done.51
  253.9 3.9 %collective-permute-start.52 = (f32[16,1,64]{2,1,0:T(1,128)S(1)}, f32[16,1,64]{2,1,0:T(1,128)S(1)}, u32[]{:S(2)}, u32[]{:S(2)}) collective-permute-start(f32[16,1,64]{2,1,0:T(1,128)S(1)} %get-tuple-element.185), channel_id=1, source_target_pairs={{8,0},{16,8},{24,16},{0,24},{9,1},{17,9},{25,17},{1,25},{10,2},{18... | collective-permute-start | bytes 12296 | tf_op jit(solution)/shard_map/ppermute | solution.py:27
  260.0 2.3 collective-permute-done.54
  265.8 2.8 collective-permute-start.56
  270.9 2.2 collective-permute-done.58
  273.1 2.1 collective-permute-done.59
  276.8 2.7 collective-permute-start.60
  281.7 2.1 collective-permute-done.62
  283.9 2.2 collective-permute-done.63
  287.2 3.9 %collective-permute-start.64 = (f32[32,1,128]{2,0,1:T(8,128)S(1)}, f32[32,1,128]{2,0,1:T(8,128)S(1)}, u32[]{:S(2)}, u32[]{:S(2)}) collective-permute-start(f32[32,1,128]{2,0,1:T(8,128)S(1)} %get-tuple-element.68), channel_id=1, source_target_pairs={{8,0},{16,8},{24,16},{0,24},{9,1},{17,9},{25,17},{1,25},{10,2},{18... | collective-permute-start | bytes 49160 | tf_op jit(solution)/shard_map/ppermute | solution.py:27
  292.6 4.1 %collective-permute-done.65 = f32[32,1,128]{2,0,1:T(8,128)S(1)} collective-permute-done((f32[32,1,128]{2,0,1:T(8,128)S(1)}, f32[32,1,128]{2,0,1:T(8,128)S(1)}, u32[]{:S(2)}, u32[]{:S(2)}) %collective-permute-start.65) | collective-permute-done | bytes 16416 | tf_op jit(solution)/shard_map/ppermute | solution.py:24
  297.5 6.7 %collective-permute-done.66 = f32[32,18,1]{2,0,1:T(8,128)S(1)} collective-permute-done((f32[32,18,1]{2,0,1:T(8,128)S(1)}, f32[32,18,1]{2,0,1:T(8,128)S(1)}, u32[]{:S(2)}, u32[]{:S(2)}) %collective-permute-start.66) | collective-permute-done | bytes 2336 | tf_op jit(solution)/shard_map/ppermute | solution.py:27
  312.2 7.3 %collective-permute-done.70 = f32[32,18,1]{2,0,1:T(8,128)S(1)} collective-permute-done((f32[32,18,1]{2,0,1:T(8,128)S(1)}, f32[32,18,1]{2,0,1:T(8,128)S(1)}, u32[]{:S(2)}, u32[]{:S(2)}) %collective-permute-start.70) | collective-permute-done | bytes 2336 | tf_op jit(solution)/shard_map/ppermute | solution.py:27
  320.7 2.0 collective-permute-start.73
  327.8 7.3 %collective-permute-done.74 = f32[32,18,1]{2,0,1:T(8,128)S(1)} collective-permute-done((f32[32,18,1]{2,0,1:T(8,128)S(1)}, f32[32,18,1]{2,0,1:T(8,128)S(1)}, u32[]{:S(2)}, u32[]{:S(2)}) %collective-permute-start.74) | collective-permute-done | bytes 2336 | tf_op jit(solution)/shard_map/ppermute | solution.py:27
  343.5 7.3 %collective-permute-done.78 = f32[32,18,1]{2,0,1:T(8,128)S(1)} collective-permute-done((f32[32,18,1]{2,0,1:T(8,128)S(1)}, f32[32,18,1]{2,0,1:T(8,128)S(1)}, u32[]{:S(2)}, u32[]{:S(2)}) %collective-permute-start.78) | collective-permute-done | bytes 2336 | tf_op jit(solution)/shard_map/ppermute | solution.py:27
  360.0 6.3 %collective-permute-done.82 = f32[32,18,1]{2,0,1:T(8,128)S(1)} collective-permute-done((f32[32,18,1]{2,0,1:T(8,128)S(1)}, f32[32,18,1]{2,0,1:T(8,128)S(1)}, u32[]{:S(2)}, u32[]{:S(2)}) %collective-permute-start.82) | collective-permute-done | bytes 2336 | tf_op jit(solution)/shard_map/ppermute | solution.py:27
  (501 shorter events, 127.2 us)
Async XLA Ops:
  0.6 17.1 %collective-permute-start.8 = (f32[32,1,128]{2,0,1:T(8,128)S(1)}, f32[32,1,128]{2,0,1:T(8,128)S(1)}, u32[]{:S(2)}, u32[]{:S(2)}) collective-permute-start(f32[32,1,128]{2,0,1:T(8,128)S(1)} %broadcast.525), channel_id=1, source_target_pairs={{8,0},{16,8},{24,16},{0,24},{9,1},{17,9},{25,17},{1,25},{10,2},{18... | collective-permute-start | bytes 49160 | tf_op jit(solution)/shard_map/ppermute | solution.py:27
  5.8 11.9 %collective-permute-start.9 = (f32[32,1,128]{2,0,1:T(8,128)S(1)}, f32[32,1,128]{2,0,1:T(8,128)S(1)}, u32[]{:S(2)}, u32[]{:S(2)}) collective-permute-start(f32[32,1,128]{2,0,1:T(8,128)S(1)} %broadcast.525), channel_id=1, source_target_pairs={{0,8},{8,16},{16,24},{24,0},{1,9},{9,17},{17,25},{25,1},{2,10},{10... | collective-permute-start | bytes 49160 | tf_op jit(solution)/shard_map/ppermute | solution.py:24
  7.2 10.6 %collective-permute-start = (f32[96,1,128]{2,0,1:T(8,128)S(1)}, f32[96,1,128]{2,0,1:T(8,128)S(1)}, u32[]{:S(2)}, u32[]{:S(2)}) collective-permute-start(f32[96,1,128]{2,0,1:T(8,128)S(1)} %get-tuple-element.23), channel_id=1, source_target_pairs={{0,8},{8,16},{16,24},{24,0},{1,9},{9,17},{17,25},{25,1},{2,10},{10... | collective-permute-start | bytes 147464 | tf_op jit(solution)/shard_map/ppermute | solution.py:24
  7.3 10.5 %collective-permute-start.1 = (f32[96,1,128]{2,0,1:T(8,128)S(1)}, f32[96,1,128]{2,0,1:T(8,128)S(1)}, u32[]{:S(2)}, u32[]{:S(2)}) collective-permute-start(f32[96,1,128]{2,0,1:T(8,128)S(1)} %get-tuple-element.24), channel_id=1, source_target_pairs={{8,0},{16,8},{24,16},{0,24},{9,1},{17,9},{25,17},{1,25},{10,2},{18... | collective-permute-start | bytes 147464 | tf_op jit(solution)/shard_map/ppermute | solution.py:27
  25.0 10.0 %collective-permute-start.10 = (f32[32,18,1]{2,0,1:T(8,128)}, f32[32,18,1]{2,0,1:T(8,128)}, u32[]{:S(2)}, u32[]{:S(2)}) collective-permute-start(f32[32,18,1]{2,0,1:T(8,128)} %get-tuple-element.47), channel_id=1, source_target_pairs={{1,0},{2,1},{3,2},{4,3},{5,4},{6,5},{7,6},{0,7},{9,8},{10,9},{11,1... | collective-permute-start | bytes 6920 | tf_op jit(solution)/shard_map/ppermute | solution.py:27
  25.0 10.1 %collective-permute-start.11 = (f32[32,18,1]{2,0,1:T(8,128)}, f32[32,18,1]{2,0,1:T(8,128)}, u32[]{:S(2)}, u32[]{:S(2)}) collective-permute-start(f32[32,18,1]{2,0,1:T(8,128)} %get-tuple-element.48), channel_id=1, source_target_pairs={{0,1},{1,2},{2,3},{3,4},{4,5},{5,6},{6,7},{7,0},{8,9},{9,10},{10,1... | collective-permute-start | bytes 6920 | tf_op jit(solution)/shard_map/ppermute | solution.py:24
  30.7 8.2 %collective-permute-start.6 = (f32[32,16,1]{2,0,1:T(8,128)S(1)}, f32[32,16,1]{2,0,1:T(8,128)S(1)}, u32[]{:S(2)}, u32[]{:S(2)}) collective-permute-start(f32[32,16,1]{2,0,1:T(8,128)S(1)} %get-tuple-element.87), channel_id=1, source_target_pairs={{1,0},{2,1},{3,2},{4,3},{5,4},{6,5},{7,6},{0,7},{9,8},{10,9},{11,1... | collective-permute-start | bytes 6152 | tf_op jit(solution)/shard_map/ppermute | solution.py:27
  33.0 7.8 %collective-permute-start.7 = (f32[32,16,1]{2,0,1:T(8,128)S(1)}, f32[32,16,1]{2,0,1:T(8,128)S(1)}, u32[]{:S(2)}, u32[]{:S(2)}) collective-permute-start(f32[32,16,1]{2,0,1:T(8,128)S(1)} %get-tuple-element.88), channel_id=1, source_target_pairs={{0,1},{1,2},{2,3},{3,4},{4,5},{5,6},{6,7},{7,0},{8,9},{9,10},{10,1... | collective-permute-start | bytes 6152 | tf_op jit(solution)/shard_map/ppermute | solution.py:24
  33.0 7.8 %collective-permute-start.4 = (f32[32,1,128]{2,0,1:T(8,128)S(1)}, f32[32,1,128]{2,0,1:T(8,128)S(1)}, u32[]{:S(2)}, u32[]{:S(2)}) collective-permute-start(f32[32,1,128]{2,0,1:T(8,128)S(1)} %get-tuple-element.85), channel_id=1, source_target_pairs={{8,0},{16,8},{24,16},{0,24},{9,1},{17,9},{25,17},{1,25},{10,2},{18... | collective-permute-start | bytes 49160 | tf_op jit(solution)/shard_map/ppermute | solution.py:27
  35.0 5.8 %collective-permute-start.5 = (f32[32,1,128]{2,0,1:T(8,128)S(1)}, f32[32,1,128]{2,0,1:T(8,128)S(1)}, u32[]{:S(2)}, u32[]{:S(2)}) collective-permute-start(f32[32,1,128]{2,0,1:T(8,128)S(1)} %get-tuple-element.86), channel_id=1, source_target_pairs={{0,8},{8,16},{16,24},{24,0},{1,9},{9,17},{17,25},{25,1},{2,10},{10... | collective-permute-start | bytes 49160 | tf_op jit(solution)/shard_map/ppermute | solution.py:24
  35.1 26.1 %collective-permute-start.28 = (f32[16,1,64]{2,1,0:T(1,128)S(1)}, f32[16,1,64]{2,1,0:T(1,128)S(1)}, u32[]{:S(2)}, u32[]{:S(2)}) collective-permute-start(f32[16,1,64]{2,1,0:T(1,128)S(1)} %broadcast.529), channel_id=1, source_target_pairs={{8,0},{16,8},{24,16},{0,24},{9,1},{17,9},{25,17},{1,25},{10,2},{18... | collective-permute-start | bytes 12296 | tf_op jit(solution)/shard_map/ppermute | solution.py:27
  38.9 22.3 %collective-permute-start.29 = (f32[16,1,64]{2,1,0:T(1,128)S(1)}, f32[16,1,64]{2,1,0:T(1,128)S(1)}, u32[]{:S(2)}, u32[]{:S(2)}) collective-permute-start(f32[16,1,64]{2,1,0:T(1,128)S(1)} %broadcast.529), channel_id=1, source_target_pairs={{0,8},{8,16},{16,24},{24,0},{1,9},{9,17},{17,25},{25,1},{2,10},{10... | collective-permute-start | bytes 12296 | tf_op jit(solution)/shard_map/ppermute | solution.py:24
  44.4 5.5 %collective-permute-start.13 = (f32[32,1,128]{2,0,1:T(8,128)S(1)}, f32[32,1,128]{2,0,1:T(8,128)S(1)}, u32[]{:S(2)}, u32[]{:S(2)}) collective-permute-start(f32[32,1,128]{2,0,1:T(8,128)S(1)} %get-tuple-element.83), channel_id=1, source_target_pairs={{0,8},{8,16},{16,24},{24,0},{1,9},{9,17},{17,25},{25,1},{2,10},{10... | collective-permute-start | bytes 49160 | tf_op jit(solution)/shard_map/ppermute | solution.py:24
  50.2 7.5 %collective-permute-start.14 = (f32[32,18,1]{2,0,1:T(8,128)S(1)}, f32[32,18,1]{2,0,1:T(8,128)S(1)}, u32[]{:S(2)}, u32[]{:S(2)}) collective-permute-start(f32[32,18,1]{2,0,1:T(8,128)S(1)} %get-tuple-element.45), channel_id=1, source_target_pairs={{1,0},{2,1},{3,2},{4,3},{5,4},{6,5},{7,6},{0,7},{9,8},{10,9},{11,1... | collective-permute-start | bytes 6920 | tf_op jit(solution)/shard_map/ppermute | solution.py:27
  51.2 7.5 %collective-permute-start.15 = (f32[32,18,1]{2,0,1:T(8,128)S(1)}, f32[32,18,1]{2,0,1:T(8,128)S(1)}, u32[]{:S(2)}, u32[]{:S(2)}) collective-permute-start(f32[32,18,1]{2,0,1:T(8,128)S(1)} %get-tuple-element.46), channel_id=1, source_target_pairs={{0,1},{1,2},{2,3},{3,4},{4,5},{5,6},{6,7},{7,0},{8,9},{9,10},{10,1... | collective-permute-start | bytes 6920 | tf_op jit(solution)/shard_map/ppermute | solution.py:24
  59.2 5.6 %collective-permute-start.17 = (f32[32,1,128]{2,0,1:T(8,128)S(1)}, f32[32,1,128]{2,0,1:T(8,128)S(1)}, u32[]{:S(2)}, u32[]{:S(2)}) collective-permute-start(f32[32,1,128]{2,0,1:T(8,128)S(1)} %get-tuple-element.79), channel_id=1, source_target_pairs={{0,8},{8,16},{16,24},{24,0},{1,9},{9,17},{17,25},{25,1},{2,10},{10... | collective-permute-start | bytes 49160 | tf_op jit(solution)/shard_map/ppermute | solution.py:24
  64.9 7.3 %collective-permute-start.18 = (f32[32,18,1]{2,0,1:T(8,128)S(1)}, f32[32,18,1]{2,0,1:T(8,128)S(1)}, u32[]{:S(2)}, u32[]{:S(2)}) collective-permute-start(f32[32,18,1]{2,0,1:T(8,128)S(1)} %get-tuple-element.43), channel_id=1, source_target_pairs={{1,0},{2,1},{3,2},{4,3},{5,4},{6,5},{7,6},{0,7},{9,8},{10,9},{11,1... | collective-permute-start | bytes 6920 | tf_op jit(solution)/shard_map/ppermute | solution.py:27
  65.7 8.1 %collective-permute-start.19 = (f32[32,18,1]{2,0,1:T(8,128)S(1)}, f32[32,18,1]{2,0,1:T(8,128)S(1)}, u32[]{:S(2)}, u32[]{:S(2)}) collective-permute-start(f32[32,18,1]{2,0,1:T(8,128)S(1)} %get-tuple-element.44), channel_id=1, source_target_pairs={{0,1},{1,2},{2,3},{3,4},{4,5},{5,6},{6,7},{7,0},{8,9},{9,10},{10,1... | collective-permute-start | bytes 6920 | tf_op jit(solution)/shard_map/ppermute | solution.py:24
  74.3 5.6 %collective-permute-start.21 = (f32[32,1,128]{2,0,1:T(8,128)S(1)}, f32[32,1,128]{2,0,1:T(8,128)S(1)}, u32[]{:S(2)}, u32[]{:S(2)}) collective-permute-start(f32[32,1,128]{2,0,1:T(8,128)S(1)} %get-tuple-element.75), channel_id=1, source_target_pairs={{0,8},{8,16},{16,24},{24,0},{1,9},{9,17},{17,25},{25,1},{2,10},{10... | collective-permute-start | bytes 49160 | tf_op jit(solution)/shard_map/ppermute | solution.py:24
  76.4 14.9 %collective-permute-start.30 = (f32[16,10,1]{2,0,1:T(8,128)S(1)}, f32[16,10,1]{2,0,1:T(8,128)S(1)}, u32[]{:S(2)}, u32[]{:S(2)}) collective-permute-start(f32[16,10,1]{2,0,1:T(8,128)S(1)} %get-tuple-element.173), channel_id=1, source_target_pairs={{1,0},{2,1},{3,2},{4,3},{5,4},{6,5},{7,6},{0,7},{9,8},{10,9},{11,1... | collective-permute-start | bytes 1928 | tf_op jit(solution)/shard_map/ppermute | solution.py:27
  77.1 14.2 %collective-permute-start.31 = (f32[16,10,1]{2,0,1:T(8,128)S(1)}, f32[16,10,1]{2,0,1:T(8,128)S(1)}, u32[]{:S(2)}, u32[]{:S(2)}) collective-permute-start(f32[16,10,1]{2,0,1:T(8,128)S(1)} %get-tuple-element.174), channel_id=1, source_target_pairs={{0,1},{1,2},{2,3},{3,4},{4,5},{5,6},{6,7},{7,0},{8,9},{9,10},{10,1... | collective-permute-start | bytes 1928 | tf_op jit(solution)/shard_map/ppermute | solution.py:24
  80.0 7.3 %collective-permute-start.22 = (f32[32,18,1]{2,0,1:T(8,128)S(1)}, f32[32,18,1]{2,0,1:T(8,128)S(1)}, u32[]{:S(2)}, u32[]{:S(2)}) collective-permute-start(f32[32,18,1]{2,0,1:T(8,128)S(1)} %get-tuple-element.41), channel_id=1, source_target_pairs={{1,0},{2,1},{3,2},{4,3},{5,4},{6,5},{7,6},{0,7},{9,8},{10,9},{11,1... | collective-permute-start | bytes 6920 | tf_op jit(solution)/shard_map/ppermute | solution.py:27
  80.2 8.7 %collective-permute-start.23 = (f32[32,18,1]{2,0,1:T(8,128)S(1)}, f32[32,18,1]{2,0,1:T(8,128)S(1)}, u32[]{:S(2)}, u32[]{:S(2)}) collective-permute-start(f32[32,18,1]{2,0,1:T(8,128)S(1)} %get-tuple-element.42), channel_id=1, source_target_pairs={{0,1},{1,2},{2,3},{3,4},{4,5},{5,6},{6,7},{7,0},{8,9},{9,10},{10,1... | collective-permute-start | bytes 6920 | tf_op jit(solution)/shard_map/ppermute | solution.py:24
  90.4 5.5 %collective-permute-start.25 = (f32[32,1,128]{2,0,1:T(8,128)S(1)}, f32[32,1,128]{2,0,1:T(8,128)S(1)}, u32[]{:S(2)}, u32[]{:S(2)}) collective-permute-start(f32[32,1,128]{2,0,1:T(8,128)S(1)} %get-tuple-element.71), channel_id=1, source_target_pairs={{0,8},{8,16},{16,24},{24,0},{1,9},{9,17},{17,25},{25,1},{2,10},{10... | collective-permute-start | bytes 49160 | tf_op jit(solution)/shard_map/ppermute | solution.py:24
  96.1 7.3 %collective-permute-start.26 = (f32[32,18,1]{2,0,1:T(8,128)S(1)}, f32[32,18,1]{2,0,1:T(8,128)S(1)}, u32[]{:S(2)}, u32[]{:S(2)}) collective-permute-start(f32[32,18,1]{2,0,1:T(8,128)S(1)} %get-tuple-element.39), channel_id=1, source_target_pairs={{1,0},{2,1},{3,2},{4,3},{5,4},{6,5},{7,6},{0,7},{9,8},{10,9},{11,1... | collective-permute-start | bytes 6920 | tf_op jit(solution)/shard_map/ppermute | solution.py:27
  96.2 7.9 %collective-permute-start.27 = (f32[32,18,1]{2,0,1:T(8,128)S(1)}, f32[32,18,1]{2,0,1:T(8,128)S(1)}, u32[]{:S(2)}, u32[]{:S(2)}) collective-permute-start(f32[32,18,1]{2,0,1:T(8,128)S(1)} %get-tuple-element.40), channel_id=1, source_target_pairs={{0,1},{1,2},{2,3},{3,4},{4,5},{5,6},{6,7},{7,0},{8,9},{9,10},{10,1... | collective-permute-start | bytes 6920 | tf_op jit(solution)/shard_map/ppermute | solution.py:24
  129.7 5.5 %collective-permute-start.33 = (f32[16,1,64]{2,1,0:T(1,128)S(1)}, f32[16,1,64]{2,1,0:T(1,128)S(1)}, u32[]{:S(2)}, u32[]{:S(2)}) collective-permute-start(f32[16,1,64]{2,1,0:T(1,128)S(1)} %get-tuple-element.206), channel_id=1, source_target_pairs={{0,8},{8,16},{16,24},{24,0},{1,9},{9,17},{17,25},{25,1},{2,10},{10... | collective-permute-start | bytes 12296 | tf_op jit(solution)/shard_map/ppermute | solution.py:24
  141.4 5.5 %collective-permute-start.37 = (f32[16,1,64]{2,1,0:T(1,128)S(1)}, f32[16,1,64]{2,1,0:T(1,128)S(1)}, u32[]{:S(2)}, u32[]{:S(2)}) collective-permute-start(f32[16,1,64]{2,1,0:T(1,128)S(1)} %get-tuple-element.202), channel_id=1, source_target_pairs={{0,8},{8,16},{16,24},{24,0},{1,9},{9,17},{17,25},{25,1},{2,10},{10... | collective-permute-start | bytes 12296 | tf_op jit(solution)/shard_map/ppermute | solution.py:24
  152.2 5.5 %collective-permute-start.41 = (f32[16,1,64]{2,1,0:T(1,128)S(1)}, f32[16,1,64]{2,1,0:T(1,128)S(1)}, u32[]{:S(2)}, u32[]{:S(2)}) collective-permute-start(f32[16,1,64]{2,1,0:T(1,128)S(1)} %get-tuple-element.198), channel_id=1, source_target_pairs={{0,8},{8,16},{16,24},{24,0},{1,9},{9,17},{17,25},{25,1},{2,10},{10... | collective-permute-start | bytes 12296 | tf_op jit(solution)/shard_map/ppermute | solution.py:24
  163.0 5.6 %collective-permute-start.45 = (f32[16,1,64]{2,1,0:T(1,128)S(1)}, f32[16,1,64]{2,1,0:T(1,128)S(1)}, u32[]{:S(2)}, u32[]{:S(2)}) collective-permute-start(f32[16,1,64]{2,1,0:T(1,128)S(1)} %get-tuple-element.194), channel_id=1, source_target_pairs={{0,8},{8,16},{16,24},{24,0},{1,9},{9,17},{17,25},{25,1},{2,10},{10... | collective-permute-start | bytes 12296 | tf_op jit(solution)/shard_map/ppermute | solution.py:24
  253.9 5.5 %collective-permute-start.53 = (f32[16,1,64]{2,1,0:T(1,128)S(1)}, f32[16,1,64]{2,1,0:T(1,128)S(1)}, u32[]{:S(2)}, u32[]{:S(2)}) collective-permute-start(f32[16,1,64]{2,1,0:T(1,128)S(1)} %get-tuple-element.186), channel_id=1, source_target_pairs={{0,8},{8,16},{16,24},{24,0},{1,9},{9,17},{17,25},{25,1},{2,10},{10... | collective-permute-start | bytes 12296 | tf_op jit(solution)/shard_map/ppermute | solution.py:24
  264.6 5.6 %collective-permute-start.57 = (f32[16,1,64]{2,1,0:T(1,128)S(1)}, f32[16,1,64]{2,1,0:T(1,128)S(1)}, u32[]{:S(2)}, u32[]{:S(2)}) collective-permute-start(f32[16,1,64]{2,1,0:T(1,128)S(1)} %get-tuple-element.182), channel_id=1, source_target_pairs={{0,8},{8,16},{16,24},{24,0},{1,9},{9,17},{17,25},{25,1},{2,10},{10... | collective-permute-start | bytes 12296 | tf_op jit(solution)/shard_map/ppermute | solution.py:24
  275.5 5.6 %collective-permute-start.61 = (f32[16,1,64]{2,1,0:T(1,128)S(1)}, f32[16,1,64]{2,1,0:T(1,128)S(1)}, u32[]{:S(2)}, u32[]{:S(2)}) collective-permute-start(f32[16,1,64]{2,1,0:T(1,128)S(1)} %get-tuple-element.178), channel_id=1, source_target_pairs={{0,8},{8,16},{16,24},{24,0},{1,9},{9,17},{17,25},{25,1},{2,10},{10... | collective-permute-start | bytes 12296 | tf_op jit(solution)/shard_map/ppermute | solution.py:24
  291.2 5.5 %collective-permute-start.65 = (f32[32,1,128]{2,0,1:T(8,128)S(1)}, f32[32,1,128]{2,0,1:T(8,128)S(1)}, u32[]{:S(2)}, u32[]{:S(2)}) collective-permute-start(f32[32,1,128]{2,0,1:T(8,128)S(1)} %get-tuple-element.67), channel_id=1, source_target_pairs={{0,8},{8,16},{16,24},{24,0},{1,9},{9,17},{17,25},{25,1},{2,10},{10... | collective-permute-start | bytes 49160 | tf_op jit(solution)/shard_map/ppermute | solution.py:24
  296.9 7.3 %collective-permute-start.66 = (f32[32,18,1]{2,0,1:T(8,128)S(1)}, f32[32,18,1]{2,0,1:T(8,128)S(1)}, u32[]{:S(2)}, u32[]{:S(2)}) collective-permute-start(f32[32,18,1]{2,0,1:T(8,128)S(1)} %get-tuple-element.37), channel_id=1, source_target_pairs={{1,0},{2,1},{3,2},{4,3},{5,4},{6,5},{7,6},{0,7},{9,8},{10,9},{11,1... | collective-permute-start | bytes 6920 | tf_op jit(solution)/shard_map/ppermute | solution.py:27
  296.9 7.8 %collective-permute-start.67 = (f32[32,18,1]{2,0,1:T(8,128)S(1)}, f32[32,18,1]{2,0,1:T(8,128)S(1)}, u32[]{:S(2)}, u32[]{:S(2)}) collective-permute-start(f32[32,18,1]{2,0,1:T(8,128)S(1)} %get-tuple-element.38), channel_id=1, source_target_pairs={{0,1},{1,2},{2,3},{3,4},{4,5},{5,6},{6,7},{7,0},{8,9},{9,10},{10,1... | collective-permute-start | bytes 6920 | tf_op jit(solution)/shard_map/ppermute | solution.py:24
  305.2 5.6 %collective-permute-start.69 = (f32[32,1,128]{2,0,1:T(8,128)S(1)}, f32[32,1,128]{2,0,1:T(8,128)S(1)}, u32[]{:S(2)}, u32[]{:S(2)}) collective-permute-start(f32[32,1,128]{2,0,1:T(8,128)S(1)} %get-tuple-element.63), channel_id=1, source_target_pairs={{0,8},{8,16},{16,24},{24,0},{1,9},{9,17},{17,25},{25,1},{2,10},{10... | collective-permute-start | bytes 49160 | tf_op jit(solution)/shard_map/ppermute | solution.py:24
  311.0 8.5 %collective-permute-start.70 = (f32[32,18,1]{2,0,1:T(8,128)S(1)}, f32[32,18,1]{2,0,1:T(8,128)S(1)}, u32[]{:S(2)}, u32[]{:S(2)}) collective-permute-start(f32[32,18,1]{2,0,1:T(8,128)S(1)} %get-tuple-element.35), channel_id=1, source_target_pairs={{1,0},{2,1},{3,2},{4,3},{5,4},{6,5},{7,6},{0,7},{9,8},{10,9},{11,1... | collective-permute-start | bytes 6920 | tf_op jit(solution)/shard_map/ppermute | solution.py:27
  312.1 8.1 %collective-permute-start.71 = (f32[32,18,1]{2,0,1:T(8,128)S(1)}, f32[32,18,1]{2,0,1:T(8,128)S(1)}, u32[]{:S(2)}, u32[]{:S(2)}) collective-permute-start(f32[32,18,1]{2,0,1:T(8,128)S(1)} %get-tuple-element.36), channel_id=1, source_target_pairs={{0,1},{1,2},{2,3},{3,4},{4,5},{5,6},{6,7},{7,0},{8,9},{9,10},{10,1... | collective-permute-start | bytes 6920 | tf_op jit(solution)/shard_map/ppermute | solution.py:24
  320.7 5.6 %collective-permute-start.73 = (f32[32,1,128]{2,0,1:T(8,128)S(1)}, f32[32,1,128]{2,0,1:T(8,128)S(1)}, u32[]{:S(2)}, u32[]{:S(2)}) collective-permute-start(f32[32,1,128]{2,0,1:T(8,128)S(1)} %get-tuple-element.59), channel_id=1, source_target_pairs={{0,8},{8,16},{16,24},{24,0},{1,9},{9,17},{17,25},{25,1},{2,10},{10... | collective-permute-start | bytes 49160 | tf_op jit(solution)/shard_map/ppermute | solution.py:24
  326.5 8.5 %collective-permute-start.74 = (f32[32,18,1]{2,0,1:T(8,128)S(1)}, f32[32,18,1]{2,0,1:T(8,128)S(1)}, u32[]{:S(2)}, u32[]{:S(2)}) collective-permute-start(f32[32,18,1]{2,0,1:T(8,128)S(1)} %get-tuple-element.33), channel_id=1, source_target_pairs={{1,0},{2,1},{3,2},{4,3},{5,4},{6,5},{7,6},{0,7},{9,8},{10,9},{11,1... | collective-permute-start | bytes 6920 | tf_op jit(solution)/shard_map/ppermute | solution.py:27
  327.7 8.1 %collective-permute-start.75 = (f32[32,18,1]{2,0,1:T(8,128)S(1)}, f32[32,18,1]{2,0,1:T(8,128)S(1)}, u32[]{:S(2)}, u32[]{:S(2)}) collective-permute-start(f32[32,18,1]{2,0,1:T(8,128)S(1)} %get-tuple-element.34), channel_id=1, source_target_pairs={{0,1},{1,2},{2,3},{3,4},{4,5},{5,6},{6,7},{7,0},{8,9},{9,10},{10,1... | collective-permute-start | bytes 6920 | tf_op jit(solution)/shard_map/ppermute | solution.py:24
  336.3 5.6 %collective-permute-start.77 = (f32[32,1,128]{2,0,1:T(8,128)S(1)}, f32[32,1,128]{2,0,1:T(8,128)S(1)}, u32[]{:S(2)}, u32[]{:S(2)}) collective-permute-start(f32[32,1,128]{2,0,1:T(8,128)S(1)} %get-tuple-element.55), channel_id=1, source_target_pairs={{0,8},{8,16},{16,24},{24,0},{1,9},{9,17},{17,25},{25,1},{2,10},{10... | collective-permute-start | bytes 49160 | tf_op jit(solution)/shard_map/ppermute | solution.py:24
  342.1 8.7 %collective-permute-start.78 = (f32[32,18,1]{2,0,1:T(8,128)S(1)}, f32[32,18,1]{2,0,1:T(8,128)S(1)}, u32[]{:S(2)}, u32[]{:S(2)}) collective-permute-start(f32[32,18,1]{2,0,1:T(8,128)S(1)} %get-tuple-element.31), channel_id=1, source_target_pairs={{1,0},{2,1},{3,2},{4,3},{5,4},{6,5},{7,6},{0,7},{9,8},{10,9},{11,1... | collective-permute-start | bytes 6920 | tf_op jit(solution)/shard_map/ppermute | solution.py:27
  343.4 8.2 %collective-permute-start.79 = (f32[32,18,1]{2,0,1:T(8,128)S(1)}, f32[32,18,1]{2,0,1:T(8,128)S(1)}, u32[]{:S(2)}, u32[]{:S(2)}) collective-permute-start(f32[32,18,1]{2,0,1:T(8,128)S(1)} %get-tuple-element.32), channel_id=1, source_target_pairs={{0,1},{1,2},{2,3},{3,4},{4,5},{5,6},{6,7},{7,0},{8,9},{9,10},{10,1... | collective-permute-start | bytes 6920 | tf_op jit(solution)/shard_map/ppermute | solution.py:24
  352.0 5.6 %collective-permute-start.81 = (f32[32,1,128]{2,0,1:T(8,128)S(1)}, f32[32,1,128]{2,0,1:T(8,128)S(1)}, u32[]{:S(2)}, u32[]{:S(2)}) collective-permute-start(f32[32,1,128]{2,0,1:T(8,128)S(1)} %get-tuple-element.49), channel_id=1, source_target_pairs={{0,8},{8,16},{16,24},{24,0},{1,9},{9,17},{17,25},{25,1},{2,10},{10... | collective-permute-start | bytes 49160 | tf_op jit(solution)/shard_map/ppermute | solution.py:24
  357.8 8.5 %collective-permute-start.82 = (f32[32,18,1]{2,0,1:T(8,128)S(1)}, f32[32,18,1]{2,0,1:T(8,128)S(1)}, u32[]{:S(2)}, u32[]{:S(2)}) collective-permute-start(f32[32,18,1]{2,0,1:T(8,128)S(1)} %get-tuple-element.29), channel_id=1, source_target_pairs={{1,0},{2,1},{3,2},{4,3},{5,4},{6,5},{7,6},{0,7},{9,8},{10,9},{11,1... | collective-permute-start | bytes 6920 | tf_op jit(solution)/shard_map/ppermute | solution.py:27
  359.1 8.1 %collective-permute-start.83 = (f32[32,18,1]{2,0,1:T(8,128)S(1)}, f32[32,18,1]{2,0,1:T(8,128)S(1)}, u32[]{:S(2)}, u32[]{:S(2)}) collective-permute-start(f32[32,18,1]{2,0,1:T(8,128)S(1)} %get-tuple-element.30), channel_id=1, source_target_pairs={{0,1},{1,2},{2,3},{3,4},{4,5},{5,6},{6,7},{7,0},{8,9},{9,10},{10,1... | collective-permute-start | bytes 6920 | tf_op jit(solution)/shard_map/ppermute | solution.py:24
  (71 other events, 696.2 us)
where the time goes:
time: 369 us
  waiting for transfers between devices  153 us (41%)
  starting transfers between devices  86.5 us (23%)
  local copies, waits for them, and re-layouts  54.2 us (15%)
  blocking collectives  42 us (11%)
  other arithmetic  30.4 us (8%)
    ppermute x42, waiting for transfers between devices, extended_2(): lax.ppermute(lax.slice_in_dim(block, 0, width, axis=dim), axis, backward)  93.4 us
    ppermute x42, starting transfers between devices, extended_2(): lax.ppermute(lax.slice_in_dim(block, 0, width, axis=dim), axis, backward)  63 us
    ppermute x42, waiting for transfers between devices, extended_2(): lax.ppermute(lax.slice_in_dim(block, block.shape[dim] - width, None, axis...  59.5 us
    all_gather x1, blocking collectives, agglomerated(): stacked = lax.all_gather(source[None], ('gx', 'gy'), axis=0, tiled=True)  42 us
    reshape x3, local copies, waits for them, and re-layouts, restrict(): field.reshape(size_z // 2, 2, size_x // 2, 2, size_y // 2, 2)  30.8 us
    ppermute x42, starting transfers between devices, extended_2(): lax.ppermute(lax.slice_in_dim(block, block.shape[dim] - width, None, axis...  23.5 us
    reduce_sum x3, other arithmetic, restrict(): field.reshape(size_z // 2, 2, size_x // 2, 2, size_y // 2, 2)  11.3 us
  transfers between devices with their start and end apart: 84, of which 61 were waited for; matrix products, arithmetic and copies ran while one was open for 6% of the time, Pallas kernels for 0%

commit v1 on v0

v1 whole, which is shorter than its diff:
```python
import functools

import jax
import jax.numpy as jnp
from jax import lax
from jax.experimental import pallas as pl
from jax.experimental.pallas import tpu as pltpu
from jax.sharding import PartitionSpec as P

LEVELS = 3
SWEEPS = 2
COARSE_SWEEPS = 8
VISCOSITY = 0.1
TIME_STEP = 0.25
WEIGHT_NEW = 15.0 / 16.0
WEIGHT_OLD = -25.0 / 48.0
HELMHOLTZ = 0.0001

LANES = 128
SUB = 8
HALO_X = 8
HALO_Y = 24
MESH = pl.DeviceIdType.MESH


def iota2(shape, dim):
    return lax.broadcasted_iota(jnp.int32, shape, dim)


def restrict_matrix(rows, cols, nz, period):
    i, o = iota2((rows, cols), 0), iota2((rows, cols), 1)
    o = o % period
    half = nz // 2
    hit = ((i // nz) // 2 == o // half) & ((i % nz) // 2 == o % half)
    return jnp.where(hit, 0.125, 0.0).astype(jnp.float32)


def prolong_matrix(rows, cols, nz):
    i, o = iota2((rows, cols), 0), iota2((rows, cols), 1)
    half = nz // 2
    hit = ((o // nz) // 2 == i // half) & ((o % nz) // 2 == i % half)
    return jnp.where(hit, 1.0, 0.0).astype(jnp.float32)


def mm(a, b):
    return jnp.dot(a, b, precision=lax.Precision.HIGHEST, preferred_element_type=jnp.float32)


class Level:
    def __init__(self, level, nz):
        self.nz = nz
        self.scale = 1.0 / float(4**level)
        lane = iota2((SUB, LANES), 1)
        row = iota2((SUB, LANES), 0)
        self.lane = lane
        self.row = row
        z = lane % nz
        self.not_top = z < nz - 1
        self.not_bottom = z > 0
        parity = (z + lane // nz + row) % 2
        self.colour = [parity == 0, parity == 1]
        edge = (z == 0) | (z == nz - 1)
        diag_in = HELMHOLTZ + 6.0 * self.scale
        diag_edge = HELMHOLTZ + 5.0 * self.scale
        self.diag = jnp.where(edge, diag_edge, diag_in).astype(jnp.float32)
        self.inv = jnp.where(edge, 1.0 / diag_edge, 1.0 / diag_in).astype(jnp.float32)
        self.take = jnp.where(
            edge, self.scale / diag_edge, self.scale / diag_in
        ).astype(jnp.float32)

    def x_plus(self, tiles, t):
        n = len(tiles)
        both = tiles[t] if n == 1 else jnp.where(self.lane < self.nz, tiles[(t + 1) % n], tiles[t])
        return pltpu.roll(both, LANES - self.nz, 1)

    def x_minus(self, tiles, t):
        n = len(tiles)
        last = self.lane >= LANES - self.nz
        both = tiles[t] if n == 1 else jnp.where(last, tiles[(t - 1) % n], tiles[t])
        return pltpu.roll(both, self.nz, 1)

    def y_plus(self, tile, following):
        return pltpu.roll(jnp.where(self.row == 0, following, tile), SUB - 1, 0)

    def y_minus(self, tile, previous):
        return pltpu.roll(jnp.where(self.row == SUB - 1, previous, tile), 1, 0)

    def z_plus(self, tile):
        return jnp.where(self.not_top, pltpu.roll(tile, LANES - 1, 1), 0.0)

    def z_minus(self, tile):
        return jnp.where(self.not_bottom, pltpu.roll(tile, 1, 1), 0.0)


def tile_of(t):
    return slice(t * LANES, (t + 1) * LANES)


def row_loop(tiles, unroll, body):
    while tiles % unroll:
        unroll -= 1

    def step(i, carry):
        for k in range(unroll):
            body(pl.multiple_of((i * unroll + k) * SUB, SUB))
        return carry

    lax.fori_loop(0, tiles // unroll, step, 0)


def neighbours(lv, p, r, tiles, t):
    cols = tile_of(t)
    here = tiles[t]
    up = lv.y_plus(here, p[pl.ds(r + 2 * SUB, SUB), cols])
    down = lv.y_minus(here, p[pl.ds(r, SUB), cols])
    return (
        lv.x_plus(tiles, t)
        + lv.x_minus(tiles, t)
        + up
        + down
        + lv.z_plus(here)
        + lv.z_minus(here)
    )


def wrap_rows(p):
    rows = p.shape[0]
    p[0:SUB, :] = p[rows - 2 * SUB : rows - SUB, :]
    p[rows - SUB : rows, :] = p[SUB : 2 * SUB, :]


def first_half(lv, p, f, unroll):
    def body(r):
        for t in range(p.shape[1] // LANES):
            p[pl.ds(r + SUB, SUB), tile_of(t)] = jnp.where(
                lv.colour[0], f[pl.ds(r, SUB), tile_of(t)] * lv.inv, 0.0
            )

    row_loop(f.shape[0] // SUB, unroll, body)


def half_sweep(lv, p, f, colour, unroll, wrap):
    if wrap:
        wrap_rows(p)
    count = p.shape[1] // LANES

    def body(r):
        tiles = [p[pl.ds(r + SUB, SUB), tile_of(t)] for t in range(count)]
        for t in range(count):
            total = neighbours(lv, p, r, tiles, t)
            new = f[pl.ds(r, SUB), tile_of(t)] * lv.inv + total * lv.take
            p[pl.ds(r + SUB, SUB), tile_of(t)] = jnp.where(lv.colour[colour], new, tiles[t])

    row_loop(f.shape[0] // SUB, unroll, body)


def presmooth(lv, p, f, sweeps, unroll, wrap):
    first_half(lv, p, f, unroll)
    for k in range(1, 2 * sweeps):
        half_sweep(lv, p, f, k % 2, unroll, wrap)


def postsmooth(lv, p, f, unroll, wrap):
    for k in range(2 * SWEEPS):
        half_sweep(lv, p, f, k % 2, unroll, wrap)


def residual(lv, p, f, out, first, last, unroll, wrap):
    if wrap:
        wrap_rows(p)
    count = p.shape[1] // LANES

    def body(r):
        tiles = [p[pl.ds(r + SUB, SUB), tile_of(t)] for t in range(count)]
        for t in range(first, last):
            total = neighbours(lv, p, r, tiles, t)
            out[pl.ds(r, SUB), tile_of(t - first)] = f[pl.ds(r, SUB), tile_of(t)] - (
                lv.diag * tiles[t] - lv.scale * total
            )

    row_loop(f.shape[0] // SUB, unroll, body)


def restrict_rows(value, pairs, start, count, emit):
    for t in range(value.shape[1] // LANES):
        pairs[t, 0 : value.shape[0], :] = value[:, tile_of(t)]
        emit(
            t,
            pairs[t, pl.ds(start, count, stride=2), :]
            + pairs[t, pl.ds(start + 1, count, stride=2), :],
        )


def prolong_rows(value, pairs, p, first):
    rows = value.shape[0]
    for k in range(value.shape[1] // LANES):
        t = first + k
        pairs[t, pl.ds(0, rows, stride=2), :] = value[:, tile_of(k)]
        pairs[t, pl.ds(1, rows, stride=2), :] = value[:, tile_of(k)]
        p[SUB : SUB + 2 * rows, tile_of(t)] += pairs[t, 0 : 2 * rows, :]


def kernel(
    nx_dev, ny_dev, nz, nx, ny,
    vel_in, old_in, obs_in, cor_out, pre_out,
    vel, old, fluid, edge, edge_in, pred,
    f0, p0, r0, f1, p1, r1, f2, p2, r2, f3, p3, pairs,
    send_sem, recv_sem,
):
    gx, gy = lax.axis_index("gx"), lax.axis_index("gy")

    def device(dx, dy):
        return (lax.rem(gx + dx + nx_dev, nx_dev), lax.rem(gy + dy + ny_dev, ny_dev))

    peers = [(d, 0) for d in range(1, nx_dev)] + [(0, d) for d in range(1, ny_dev)]
    peers += [(a, b) for a in (-1, 1) for b in (-1, 1)]
    barrier = pltpu.get_barrier_semaphore()
    for dx, dy in peers:
        pl.semaphore_signal(barrier, inc=1, device_id=device(dx, dy), device_id_type=MESH)

    number = [0]

    def send(src, dst, dx, dy):
        k = number[0]
        number[0] += 1
        copy = pltpu.make_async_remote_copy(
            src_ref=src, dst_ref=dst, send_sem=send_sem.at[k], recv_sem=recv_sem.at[k],
            device_id=device(dx, dy), device_id_type=MESH,
        )
        copy.start()
        return copy

    per = LANES // nz
    blocks = nx // per
    width = blocks * LANES
    lv0 = Level(0, nz)
    lane = lv0.lane

    def load_tile(ref, base, t):
        rows = [ref[pl.ds(base + t * per + i, nz, stride=nx), :] for i in range(per)]
        return jnp.concatenate(rows, axis=0).T

    for c in range(3):
        for t in range(blocks):
            vel[c, SUB : SUB + ny, tile_of(t + 1)] = load_tile(vel_in, c * nz * nx, t)

    pltpu_wait = functools.partial(pl.semaphore_wait, barrier)
    pltpu_wait(len(peers))

    def join(high):
        parts = []
        for c in range(3):
            source = vel[c, SUB : SUB + ny, tile_of(blocks if high else 1)]
            start = LANES - nz if high else 0
            parts.append(pltpu.roll(source, (c * nz - start) % LANES, 1))
        wide = iota2((ny, LANES), 1)
        return jnp.where(wide < nz, parts[0], jnp.where(wide < 2 * nz, parts[1], parts[2]))

    copies = [
        send(vel.at[:, ny : ny + SUB, LANES : LANES + width], vel.at[:, 0:SUB, LANES : LANES + width], 0, 1),
        send(
            vel.at[:, SUB : 2 * SUB, LANES : LANES + width],
            vel.at[:, SUB + ny : 2 * SUB + ny, LANES : LANES + width], 0, -1,
        ),
    ]
    edge[0] = join(True)
    copies.append(send(edge.at[0], edge_in.at[0], 1, 0))
    edge[1] = join(False)
    copies.append(send(edge.at[1], edge_in.at[1], -1, 0))

    for c in range(3):
        for t in range(blocks):
            old[c, :, tile_of(t)] = load_tile(old_in, c * nz * nx, t)
    for t in range(blocks):
        fluid[:, tile_of(t)] = (1 - load_tile(obs_in, 0, t)).astype(jnp.float32)
    for copy in copies:
        copy.wait()
    for c in range(3):
        vel[c, SUB : SUB + ny, tile_of(0)] = pltpu.roll(edge_in[0], (LANES - nz - c * nz) % LANES, 1)
        vel[c, SUB : SUB + ny, tile_of(blocks + 1)] = pltpu.roll(edge_in[1], (-c * nz) % LANES, 1)

    def momentum(r):
        here = [
            [vel[c, pl.ds(r + SUB, SUB), tile_of(t)] for t in range(blocks + 2)] for c in range(3)
        ]
        for t in range(1, blocks + 1):
            cols = tile_of(t)
            wet = fluid[pl.ds(r, SUB), tile_of(t - 1)]
            for c in range(3):
                q = here[c][t]
                xp, xm = lv0.x_plus(here[c], t), lv0.x_minus(here[c], t)
                yp = lv0.y_plus(q, vel[c, pl.ds(r + 2 * SUB, SUB), cols])
                ym = lv0.y_minus(q, vel[c, pl.ds(r, SUB), cols])
                zp, zm = lv0.z_plus(q), lv0.z_minus(q)
                advect = 0.5 * (
                    here[0][t] * (xp - xm) + here[1][t] * (yp - ym) + here[2][t] * (zp - zm)
                )
                diffuse = xp + xm + yp + ym + zp + zm - 6.0 * q
                tendency = VISCOSITY * diffuse - advect
                pred[c, pl.ds(r + SUB, SUB), cols] = wet * (
                    q
                    + TIME_STEP
                    * (WEIGHT_NEW * tendency + WEIGHT_OLD * old[c, pl.ds(r, SUB), tile_of(t - 1)])
                )

    row_loop(ny // SUB, 1, momentum)

    inner = slice(LANES, LANES + width)
    copies = [
        send(pred.at[0, SUB : SUB + ny, tile_of(blocks)], pred.at[0, SUB : SUB + ny, tile_of(0)], 1, 0),
        send(pred.at[0, SUB : SUB + ny, tile_of(1)], pred.at[0, SUB : SUB + ny, tile_of(blocks + 1)], -1, 0),
        send(pred.at[1, ny : ny + SUB, inner], pred.at[1, 0:SUB, inner], 0, 1),
        send(pred.at[1, SUB : 2 * SUB, inner], pred.at[1, SUB + ny : 2 * SUB + ny, inner], 0, -1),
    ]
    for copy in copies:
        copy.wait()

    side = HALO_X // per
    hx = side * LANES

    def divergence(r):
        u = [pred[0, pl.ds(r + SUB, SUB), tile_of(t)] for t in range(blocks + 2)]
        for t in range(1, blocks + 1):
            cols = tile_of(t)
            v = pred[1, pl.ds(r + SUB, SUB), cols]
            w = pred[2, pl.ds(r + SUB, SUB), cols]
            v_plus = lv0.y_plus(v, pred[1, pl.ds(r + 2 * SUB, SUB), cols])
            v_minus = lv0.y_minus(v, pred[1, pl.ds(r, SUB), cols])
            total = (
                (lv0.x_plus(u, t) - lv0.x_minus(u, t))
                + (v_plus - v_minus)
                + (lv0.z_plus(w) - lv0.z_minus(w))
            )
            f0[pl.ds(r + HALO_Y, SUB), tile_of(t - 1 + side)] = total * (-0.5 / TIME_STEP)

    row_loop(ny // SUB, 1, divergence)

    span = {
        0: (slice(HALO_Y, HALO_Y + ny), slice(HALO_Y, HALO_Y + ny)),
        1: (slice(ny, ny + HALO_Y), slice(0, HALO_Y)),
        -1: (slice(HALO_Y, 2 * HALO_Y), slice(HALO_Y + ny, 2 * HALO_Y + ny)),
    }
    cross = {
        0: (slice(hx, hx + width), slice(hx, hx + width)),
        1: (slice(width, width + hx), slice(0, hx)),
        -1: (slice(hx, 2 * hx), slice(hx + width, 2 * hx + width)),
    }
    copies = []
    for dx, dy in ((1, 0), (-1, 0), (0, 1), (0, -1), (1, 1), (1, -1), (-1, 1), (-1, -1)):
        copies.append(
            send(f0.at[span[dy][0], cross[dx][0]], f0.at[span[dy][1], cross[dx][1]], dx, dy)
        )
    lv1, lv2, lv3 = Level(1, nz // 2), Level(2, nz // 4), Level(3, nz // 8)
    zero_rows = jnp.zeros((SUB, p0.shape[1]), jnp.float32)
    p0[0:SUB, :] = zero_rows
    p0[p0.shape[0] - SUB :, :] = zero_rows
    p1[0:SUB, :] = zero_rows[:, : p1.shape[1]]
    p1[p1.shape[0] - SUB :, :] = zero_rows[:, : p1.shape[1]]
    for copy in copies:
        copy.wait()

    presmooth(lv0, p0, f0, SWEEPS, 1, False)
    residual(lv0, p0, f0, r0, side, side + blocks, 1, False)
    rows1 = f1.shape[0]
    down1 = mm(r0[...], restrict_matrix(width, LANES, nz, LANES))

    def emit1(t, value):
        f1[:, tile_of(t)] = value

    restrict_rows(down1, pairs, 0, rows1, emit1)

    copies = [
        send(f1.at[:, tile_of(0)], f1.at[:, tile_of(j)], nx_dev - j, 0) for j in range(1, nx_dev)
    ]
    for copy in copies:
        copy.wait()
    presmooth(lv1, p1, f1, SWEEPS, 1, False)
    residual(lv1, p1, f1, r1, 0, nx_dev, 1, False)
    cols2 = f2.shape[1]
    down2 = mm(r1[...], restrict_matrix(r1.shape[1], cols2, nz // 2, cols2))
    own2 = ny // 4

    def emit2(t, value):
        f2[0:own2, tile_of(t)] = value

    restrict_rows(down2, pairs, HALO_Y // 2, own2, emit2)
    copies = [
        send(f2.at[0:own2, :], f2.at[j * own2 : (j + 1) * own2, :], 0, ny_dev - j)
        for j in range(1, ny_dev)
    ]
    for copy in copies:
        copy.wait()

    presmooth(lv2, p2, f2, SWEEPS, 8, True)
    residual(lv2, p2, f2, r2, 0, cols2 // LANES, 8, True)
    down3 = mm(r2[...], restrict_matrix(cols2, f3.shape[1], nz // 4, cols2 // 4))

    def emit3(t, value):
        f3[:, tile_of(t)] = value

    restrict_rows(down3, pairs, 0, f3.shape[0], emit3)
    presmooth(lv3, p3, f3, COARSE_SWEEPS, 16, True)
    rows3 = f3.shape[0]
    prolong_rows(
        mm(p3[SUB : SUB + rows3, :], prolong_matrix(p3.shape[1], cols2, nz // 4)), pairs, p2, 0
    )
    postsmooth(lv2, p2, f2, 8, True)
    wrap_rows(p2)

    first2 = SUB - HALO_Y // 4
    window = p2[first2 : first2 + rows1 // 2, :]
    prolong_rows(mm(window, prolong_matrix(cols2, r1.shape[1], nz // 2)), pairs, p1, 0)
    postsmooth(lv1, p1, f1, 1, False)

    lift = prolong_matrix(LANES, width, nz)
    body_rows = slice(SUB, SUB + rows1)
    prolong_rows(mm(p1[body_rows, tile_of(nx_dev - 1)], lift[:, width - hx :]), pairs, p0, 0)
    prolong_rows(mm(p1[body_rows, tile_of(0)], lift), pairs, p0, side)
    prolong_rows(mm(p1[body_rows, tile_of(1)], lift[:, :hx]), pairs, p0, side + blocks)
    postsmooth(lv0, p0, f0, 1, False)

    low = SUB + HALO_Y

    def correct(r):
        here = [
            p0[pl.ds(r + low, SUB), tile_of(t)] for t in range(side - 1, side + blocks + 1)
        ]
        for t in range(1, blocks + 1):
            cols = tile_of(t + side - 1)
            slope = (
                lv0.x_plus(here, t) - lv0.x_minus(here, t),
                lv0.y_plus(here[t], p0[pl.ds(r + low + SUB, SUB), cols])
                - lv0.y_minus(here[t], p0[pl.ds(r + low - SUB, SUB), cols]),
                lv0.z_plus(here[t]) - lv0.z_minus(here[t]),
            )
            wet = fluid[pl.ds(r, SUB), tile_of(t - 1)]
            for c in range(3):
                old[c, pl.ds(r, SUB), tile_of(t - 1)] = wet * (
                    pred[c, pl.ds(r + SUB, SUB), tile_of(t)] - (0.5 * TIME_STEP) * slope[c]
                )

    row_loop(ny // SUB, 1, correct)

    def store_tile(ref, base, t, value):
        turned = value.T
        for i in range(per):
            ref[pl.ds(base + t * per + i, nz, stride=nx), :] = turned[i * nz : (i + 1) * nz, :]

    for t in range(blocks):
        store_tile(pre_out, 0, t, p0[low : low + ny, tile_of(t + side)])
    for c in range(3):
        for t in range(blocks):
            store_tile(cor_out, c * nz * nx, t, old[c, :, tile_of(t)])


def body(nx_dev, ny_dev, velocity, old_tendency, obstacle):
    _, nz, nx, ny = velocity.shape
    rows0 = ny + 2 * HALO_Y
    wide0 = (nx + 2 * HALO_X) * nz
    width = nx * nz
    rows1, wide1 = rows0 // 2, nx_dev * (nx // 2) * (nz // 2)
    rows2, wide2 = ny_dev * ny // 4, nx_dev * (nx // 4) * (nz // 4)
    rows3 = rows2 // 2
    wide3 = max(LANES, wide2 // 4)
    tall = max(rows0, rows1, rows2)
    count = max(wide0, wide1, wide2, wide3) // LANES
    copies = 4 + 4 + 8 + (nx_dev - 1) + (ny_dev - 1)
    f32 = jnp.float32
    out = pl.pallas_call(
        functools.partial(kernel, nx_dev, ny_dev, nz, nx, ny),
        out_shape=(
            jax.ShapeDtypeStruct((3 * nz * nx, ny), f32),
            jax.ShapeDtypeStruct((nz * nx, ny), f32),
        ),
        in_specs=[pl.BlockSpec(memory_space=pltpu.VMEM)] * 3,
        out_specs=[pl.BlockSpec(memory_space=pltpu.VMEM)] * 2,
        scratch_shapes=[
            pltpu.VMEM((3, ny + 2 * SUB, width + 2 * LANES), f32),
            pltpu.VMEM((3, ny, width), f32),
            pltpu.VMEM((ny, width), f32),
            pltpu.VMEM((2, ny, LANES), f32),
            pltpu.VMEM((2, ny, LANES), f32),
            pltpu.VMEM((3, ny + 2 * SUB, width + 2 * LANES), f32),
            pltpu.VMEM((rows0, wide0), f32),
            pltpu.VMEM((rows0 + 2 * SUB, wide0), f32),
            pltpu.VMEM((rows0, width), f32),
            pltpu.VMEM((rows1, wide1), f32),
            pltpu.VMEM((rows1 + 2 * SUB, wide1), f32),
            pltpu.VMEM((rows1, wide1), f32),
            pltpu.VMEM((rows2, wide2), f32),
            pltpu.VMEM((rows2 + 2 * SUB, wide2), f32),
            pltpu.VMEM((rows2, wide2), f32),
            pltpu.VMEM((rows3, wide3), f32),
            pltpu.VMEM((rows3 + 2 * SUB, wide3), f32),
            pltpu.VMEM((count, tall, LANES), f32),
            pltpu.SemaphoreType.DMA((copies,)),
            pltpu.SemaphoreType.DMA((copies,)),
        ],
        compiler_params=pltpu.CompilerParams(
            collective_id=0, has_side_effects=True, vmem_limit_bytes=60 * 1024 * 1024
        ),
    )(
        velocity.reshape(3 * nz * nx, ny),
        old_tendency.reshape(3 * nz * nx, ny),
        obstacle.reshape(nz * nx, ny),
    )
    return out[0].reshape(3, nz, nx, ny), out[1].reshape(nz, nx, ny)


def solution(mesh):
    placed = (P(None, None, "gx", "gy"), P(None, None, "gx", "gy"), P(None, "gx", "gy"))
    return jax.shard_map(
        functools.partial(body, mesh.shape["gx"], mesh.shape["gy"]),
        mesh=mesh,
        in_specs=placed,
        out_specs=(P(None, None, "gx", "gy"), P(None, "gx", "gy")),
        check_vma=False,
    )
```

time: 369 us -> 90.8 us (0.25)
  waiting for transfers between devices: 153 us -> 0 us
  Pallas kernels: 0 us -> 87.2 us
  starting transfers between devices: 86.5 us -> 0 us
  local copies, waits for them, and re-layouts: 54.2 us -> 2.81 us
  blocking collectives: 42 us -> 0 us
  other arithmetic: 30.4 us -> 0 us
    ppermute x84 -> x0, waiting for transfers between devices: 153 us -> none  [the longest x42 93.4 us: extended_2(): lax.ppermute(lax.slice_in_dim(block, 0, width, axis=dim), axis, backward)]
    pallas_call x0 -> x1, Pallas kernels: none -> 87.2 us  [body(): pl.pallas_call(functools.partial(kernel, nx_dev, ny_dev, nz, nx, ny), out...]
    ppermute x84 -> x0, starting transfers between devices: 86.5 us -> none  [the longest x42 63 us: extended_2(): lax.ppermute(lax.slice_in_dim(block, 0, width, axis=dim), axis, backward)]
    all_gather x1 -> x0, blocking collectives: 42 us -> none  [agglomerated(): stacked = lax.all_gather(source[None], ('gx', 'gy'), axis=0, tiled=True)]
    reshape x10 -> x0, local copies, waits for them, and re-layouts: 32.3 us -> none  [the longest x3 30.8 us: restrict(): field.reshape(size_z // 2, 2, size_x // 2, 2, size_y // 2, 2)]
    slice x136 -> x0, local copies, waits for them, and re-layouts: 11.6 us -> none  [the longest x30 3.48 us: extended_2(): lax.slice_in_dim(block, 0, width, axis=dim)]
    reduce_sum x3 -> x0, other arithmetic: 11.3 us -> none  [restrict(): field.reshape(size_z // 2, 2, size_x // 2, 2, size_y // 2, 2)]
    select_n x40 -> x0, other arithmetic: 9.29 us -> none  [the longest x16 5.19 us: smooth(): jnp.where(colour == shade, relax_update(face_halo(field), source, spacing...]
  transfers between devices with their start and end apart: 84 -> 0, of which waited for: 61 -> 0; matrix products, arithmetic and copies ran while one was open for 6% -> 0% of each run, Pallas kernels for 0% -> 0%
where the time goes in v1:
time: 90.8 us; the launch traced here: 90.7 us
  Pallas kernels  87.2 us (96%)
  local copies, waits for them, and re-layouts  2.81 us (3%)
    pallas_call x1, Pallas kernels, body(): pl.pallas_call(functools.partial(kernel, nx_dev, ny_dev, nz, nx, ny), out...  87.2 us
    unnamed x4, local copies, waits for them, and re-layouts  2.81 us

profile of v1, /device:TPU:0, one launch (start us, length us, event | category | flops | bytes accessed | tf_op | source)
XLA Modules:
  0.0 90.7 jit_solution(16054898858324291090)
XLA Ops:
  0.6 87.2 %shard_map.50 = (f32[1536,128]{1,0:T(8,128)}, f32[512,128]{1,0:T(8,128)}) custom-call(f32[1536,128]{1,0:T(8,128)} %bitcast.5, f32[1536,128]{1,0:T(8,128)} %bitcast.6, s32[512,128]{1,0:T(8,128)} %bitcast.8), custom_call_target="tpu_custom_call" | custom-call | tf_op jit(solution)/shard_map/pallas_call | solution.py:469
  87.9 0.0 copy-start
  87.9 2.1 %copy.7 = f32[3,32,16,128]{3,2,1,0:T(8,128)} copy(f32[3,32,16,128]{3,2,1,0:T(8,128)} %bitcast.7) | data formatting | bytes 1572864
  90.0 0.0 copy-done
  90.0 0.7 copy.8
Async XLA Ops:
  87.9 2.1 %copy-start = (f32[512,128]{1,0:T(8,128)S(1)}, f32[512,128]{1,0:T(8,128)}, u32[]{:S(2)}) copy-start(f32[512,128]{1,0:T(8,128)} %get-tuple-element.5) | copy-start | bytes 786436

commit v2 on v1

--- a/solution.py
+++ b/solution.py
@@ -139,19 +139,22 @@
     row_loop(f.shape[0] // SUB, unroll, body)
 
 
-def half_sweep(lv, p, f, colour, unroll, wrap):
+def half_sweep(lv, p, f, colour, unroll, wrap, trim_rows=0, trim_tiles=0):
     if wrap:
         wrap_rows(p)
     count = p.shape[1] // LANES
 
-    def body(r):
+    def body(start):
+        r = start + trim_rows
         tiles = [p[pl.ds(r + SUB, SUB), tile_of(t)] for t in range(count)]
-        for t in range(count):
+        for t in range(trim_tiles, count - trim_tiles):
             total = neighbours(lv, p, r, tiles, t)
             new = f[pl.ds(r, SUB), tile_of(t)] * lv.inv + total * lv.take
-            p[pl.ds(r + SUB, SUB), tile_of(t)] = jnp.where(lv.colour[colour], new, tiles[t])
-
-    row_loop(f.shape[0] // SUB, unroll, body)
+            p[pl.ds(r + SUB, SUB), tile_of(t)] = (
+                jnp.where(lv.colour[0], tiles[t], new) if colour else jnp.where(lv.colour[0], new, tiles[t])
+            )
+
+    row_loop((f.shape[0] - 2 * trim_rows) // SUB, unroll, body)
 
 
 def presmooth(lv, p, f, sweeps, unroll, wrap):
@@ -160,9 +163,9 @@
         half_sweep(lv, p, f, k % 2, unroll, wrap)
 
 
-def postsmooth(lv, p, f, unroll, wrap):
+def postsmooth(lv, p, f, unroll, wrap, trim_rows=0, trim_tiles=0):
     for k in range(2 * SWEEPS):
-        half_sweep(lv, p, f, k % 2, unroll, wrap)
+        half_sweep(lv, p, f, k % 2, unroll, wrap, trim_rows, trim_tiles)
 
 
 def residual(lv, p, f, out, first, last, unroll, wrap):
@@ -303,7 +306,7 @@
                     * (WEIGHT_NEW * tendency + WEIGHT_OLD * old[c, pl.ds(r, SUB), tile_of(t - 1)])
                 )
 
-    row_loop(ny // SUB, 1, momentum)
+    row_loop(ny // SUB, 2, momentum)
 
     inner = slice(LANES, LANES + width)
     copies = [
@@ -333,7 +336,7 @@
             )
             f0[pl.ds(r + HALO_Y, SUB), tile_of(t - 1 + side)] = total * (-0.5 / TIME_STEP)
 
-    row_loop(ny // SUB, 1, divergence)
+    row_loop(ny // SUB, 2, divergence)
 
     span = {
         0: (slice(HALO_Y, HALO_Y + ny), slice(HALO_Y, HALO_Y + ny)),
@@ -359,8 +362,8 @@
     for copy in copies:
         copy.wait()
 
-    presmooth(lv0, p0, f0, SWEEPS, 1, False)
-    residual(lv0, p0, f0, r0, side, side + blocks, 1, False)
+    presmooth(lv0, p0, f0, SWEEPS, 2, False)
+    residual(lv0, p0, f0, r0, side, side + blocks, 2, False)
     rows1 = f1.shape[0]
     down1 = mm(r0[...], restrict_matrix(width, LANES, nz, LANES))
 
@@ -374,7 +377,7 @@
     ]
     for copy in copies:
         copy.wait()
-    presmooth(lv1, p1, f1, SWEEPS, 1, False)
+    presmooth(lv1, p1, f1, SWEEPS, 11, False)
     residual(lv1, p1, f1, r1, 0, nx_dev, 1, False)
     cols2 = f2.shape[1]
     down2 = mm(r1[...], restrict_matrix(r1.shape[1], cols2, nz // 2, cols2))
@@ -391,8 +394,8 @@
     for copy in copies:
         copy.wait()
 
-    presmooth(lv2, p2, f2, SWEEPS, 8, True)
-    residual(lv2, p2, f2, r2, 0, cols2 // LANES, 8, True)
+    presmooth(lv2, p2, f2, SWEEPS, 16, True)
+    residual(lv2, p2, f2, r2, 0, cols2 // LANES, 16, True)
     down3 = mm(r2[...], restrict_matrix(cols2, f3.shape[1], nz // 4, cols2 // 4))
 
     def emit3(t, value):
@@ -404,20 +407,20 @@
     prolong_rows(
         mm(p3[SUB : SUB + rows3, :], prolong_matrix(p3.shape[1], cols2, nz // 4)), pairs, p2, 0
     )
-    postsmooth(lv2, p2, f2, 8, True)
+    postsmooth(lv2, p2, f2, 16, True)
     wrap_rows(p2)
 
     first2 = SUB - HALO_Y // 4
     window = p2[first2 : first2 + rows1 // 2, :]
     prolong_rows(mm(window, prolong_matrix(cols2, r1.shape[1], nz // 2)), pairs, p1, 0)
-    postsmooth(lv1, p1, f1, 1, False)
+    postsmooth(lv1, p1, f1, 11, False)
 
     lift = prolong_matrix(LANES, width, nz)
     body_rows = slice(SUB, SUB + rows1)
     prolong_rows(mm(p1[body_rows, tile_of(nx_dev - 1)], lift[:, width - hx :]), pairs, p0, 0)
     prolong_rows(mm(p1[body_rows, tile_of(0)], lift), pairs, p0, side)
     prolong_rows(mm(p1[body_rows, tile_of(1)], lift[:, :hx]), pairs, p0, side + blocks)
-    postsmooth(lv0, p0, f0, 1, False)
+    postsmooth(lv0, p0, f0, 3, False, HALO_Y - SUB, side - 1)
 
     low = SUB + HALO_Y
 
@@ -439,7 +442,7 @@
                     pred[c, pl.ds(r + SUB, SUB), tile_of(t)] - (0.5 * TIME_STEP) * slope[c]
                 )
 
-    row_loop(ny // SUB, 1, correct)
+    row_loop(ny // SUB, 2, correct)
 
     def store_tile(ref, base, t, value):
         turned = value.T

time: 90.8 us -> 75.3 us (0.83)
  Pallas kernels: 87.2 us -> 71.6 us
    pallas_call x1, Pallas kernels: 87.2 us -> 71.6 us  [body(): pl.pallas_call(functools.partial(kernel, nx_dev, ny_dev, nz, nx, ny), out...]
where the time goes in v2:
time: 75.3 us; the launch traced here: 75.1 us
  Pallas kernels  71.6 us (95%)
  local copies, waits for them, and re-layouts  2.81 us (4%)
    pallas_call x1, Pallas kernels, body(): pl.pallas_call(functools.partial(kernel, nx_dev, ny_dev, nz, nx, ny), out...  71.6 us
    unnamed x4, local copies, waits for them, and re-layouts  2.81 us

profile of v2, /device:TPU:0, one launch (start us, length us, event | category | flops | bytes accessed | tf_op | source)
XLA Modules:
  0.0 75.1 jit_solution(16527690337368176835)
XLA Ops:
  0.6 71.6 %shard_map.50 = (f32[1536,128]{1,0:T(8,128)}, f32[512,128]{1,0:T(8,128)}) custom-call(f32[1536,128]{1,0:T(8,128)} %bitcast.5, f32[1536,128]{1,0:T(8,128)} %bitcast.6, s32[512,128]{1,0:T(8,128)} %bitcast.8), custom_call_target="tpu_custom_call" | custom-call | tf_op jit(solution)/shard_map/pallas_call | solution.py:472
  72.3 0.0 copy-start
  72.3 2.1 %copy.7 = f32[3,32,16,128]{3,2,1,0:T(8,128)} copy(f32[3,32,16,128]{3,2,1,0:T(8,128)} %bitcast.7) | data formatting | bytes 1572864
  74.4 0.0 copy-done
  74.4 0.7 copy.8
Async XLA Ops:
  72.3 2.1 %copy-start = (f32[512,128]{1,0:T(8,128)S(1)}, f32[512,128]{1,0:T(8,128)}, u32[]{:S(2)}) copy-start(f32[512,128]{1,0:T(8,128)} %get-tuple-element.5) | copy-start | bytes 786436
